TPU v7x, 32 devices: a whole 2x2x4 slice. The times are simulated.
32 devices in a mesh: row: 4 (over y, x), col: 8 (over z, core).
Axes of the slice: x: 2, y: 2, z: 4, core: 2. Of those that a mesh axis runs over, the one named last changes fastest.
Arguments:
- panel_right: bfloat16 [32, 1536, 128], P('row', 'col'), may hold values from -1 to 1
- factor_inverse: bfloat16 [1536, 1536], replicated, as said below
- ranks: int32 [32], P(('row', 'col')), may hold values from 32 to 128
- owner_map: int32 [32], replicated, may hold values from 0 to 31, each once
- cores: float32 [4, 8, 8, 4, 128, 128], P('row', 'col'), may hold values from -6 to 6
Outputs:
- new_cores: float32 [4, 8, 8, 4, 128, 128], P('row', 'col')
Inputs may be any that keep to these rules, and one draw needn't show every extreme that they name: `factor_inverse`: lower triangular, the inverse of a Cholesky factor.
All inputs are finite; a program needn't handle non-finite values.
Results may differ from a plain program's by a relative error of at most 0.0033.
Values may be sent and summed in bfloat16 or wider, within the bound.
No kernel may reach another device: no remote copies, remote signals or barrier semaphores. Data moves between devices by JAX's collectives and lax.ppermute only.
A program may use at most 128 MiB of HBM per device.

v0:
```python
import jax
import jax.numpy as jnp
from jax import lax
from jax.sharding import PartitionSpec as P


def body(panel_right, factor_inverse, ranks, owner_map, cores):
    n_row = lax.axis_size("row")
    n_col = lax.axis_size("col")
    devices = n_row * n_col
    order = factor_inverse.shape[0]
    width = panel_right.shape[2]
    whole = lax.all_to_all(panel_right, "col", split_axis=0, concat_axis=1, tiled=True)
    solved = jnp.einsum("ij,bjk->bik", factor_inverse, whole, preferred_element_type=jnp.float32)
    column = lax.broadcasted_iota(jnp.int32, (1, 1, width), 2)
    keep = column < ranks.reshape(1, 1, 1)
    panel_left = jnp.where(keep, solved, 0.0).astype(jnp.bfloat16)
    pieces = panel_left.reshape(devices, order // devices, width)
    spread = lax.all_to_all(pieces, ("row", "col"), split_axis=0, concat_axis=0, tiled=True)
    moved = jnp.take(spread, owner_map, axis=0)
    back = lax.all_to_all(moved, ("row", "col"), split_axis=0, concat_axis=0, tiled=True)
    held = back.reshape(1, order, width)
    column_set = lax.all_gather(held, "row", axis=0, tiled=True)
    gram = jnp.einsum(
        "aik,bil->abkl",
        lax.all_gather(held, "col", axis=0, tiled=True),
        column_set,
        preferred_element_type=jnp.float32,
    )
    return cores - gram[None, None]


def solution(mesh):
    return jax.shard_map(
        body,
        mesh=mesh,
        in_specs=(
            P("row", "col", None),
            P(),
            P(("row", "col")),
            P(),
            P("row", "col", None, None, None, None),
        ),
        out_specs=P("row", "col", None, None, None, None),
        check_vma=False,
    )
```

profile of v0, /device:TPU:0, one launch (start us, length us, event | category | flops | bytes accessed | tf_op | source)
XLA Modules:
  0.0 147.6 jit_solution(1991811806430617758)
XLA Ops:
  6.5 6.4 %all-to-all-start = ((bf16[8,192,128]{2,1,0:T(8,128)(2,1)}), bf16[8,192,128]{2,1,0:T(8,128)(2,1)S(1)}, u32[]{:S(2)}, u32[]{:S(2)}) async-start(bf16[8,192,128]{2,1,0:T(8,128)(2,1)} %param.5), calls=%async_computation | async-start | bytes 786432 | tf_op jit(solution)/shard_map/all_to_all | solution.py:13
  13.6 11.9 %all-to-all-done = bf16[8,192,128]{2,1,0:T(8,128)(2,1)S(1)} async-done(((bf16[8,192,128]{2,1,0:T(8,128)(2,1)}), bf16[8,192,128]{2,1,0:T(8,128)(2,1)S(1)}, u32[]{:S(2)}, u32[]{:S(2)}) %all-to-all-start) | async-done | bytes 393248 | tf_op jit(solution)/shard_map/all_to_all | solution.py:13
  25.4 0.0 copy-start
  25.4 4.0 %fusion.4 = bf16[1,1536,128]{1,2,0:T(8,128)(2,1)S(1)} fusion(bf16[1536,128]{1,0:T(8,128)(2,1)S(1)} %bitcast.33, bf16[1536,1536]{1,0:T(8,128)(2,1)} %param.6, pred[128]{0:T(512)(128)(4,1)S(1)} %iota_compare_fusion), kind=kOutput, calls=%fused_computation.6 | convolution fusion | flops 604372992 | bytes 5505152 | tf_op jit(solution)/shard_map/ij,bjk->bik/dot_general | solution.py:14
  29.4 0.9 copy.14
  30.4 3.5 %all-to-all-start.1 = ((bf16[32,48,128]{2,1,0:T(8,128)(2,1)}), bf16[32,48,128]{2,1,0:T(8,128)(2,1)S(1)}, u32[]{:S(2)}, u32[]{:S(2)}) async-start(bf16[32,48,128]{2,1,0:T(8,128)(2,1)} %bitcast.4), calls=%async_computation.1 | async-start | bytes 786432 | tf_op jit(solution)/shard_map/all_to_all | solution.py:19
  33.9 0.0 all-gather.3.cloned.1.call-start
  34.0 0.0 copy-done
  34.0 13.3 %all-to-all-done.1 = bf16[32,48,128]{2,1,0:T(8,128)(2,1)S(1)} async-done(((bf16[32,48,128]{2,1,0:T(8,128)(2,1)}), bf16[32,48,128]{2,1,0:T(8,128)(2,1)S(1)}, u32[]{:S(2)}, u32[]{:S(2)}) %all-to-all-start.1) | async-done | bytes 393248 | tf_op jit(solution)/shard_map/all_to_all | solution.py:19
  47.3 0.6 gather_fusion
  48.0 0.1 broadcast_select_fusion
  48.1 15.8 %all_to_all.19 = bf16[32,48,128]{2,1,0:T(8,128)(2,1)} all-to-all(bf16[32,48,128]{2,1,0:T(8,128)(2,1)S(1)} %broadcast_select_fusion), channel_id=1, replica_groups=mesh['row'=4,'col'=8] {'row','col'}, dimensions={0} | all-to-all | bytes 786432 | tf_op jit(solution)/shard_map/all_to_all | solution.py:21
  63.9 0.0 all-gather.3.cloned.1.call-update
  63.9 0.0 all-gather.5.cloned.1.call-start
  64.0 0.7 all-gather.5.cloned.1.call-update
  64.7 1.9 %copy.16 = f32[1,1,8,4,128,128]{4,5,2,3,1,0:T(8,128)S(1)} copy(f32[1,1,8,4,128,128]{5,4,3,2,1,0:T(8,128)} %param.9) | data formatting | bytes 4194304 | tf_op args[4]
  66.6 25.9 %all-gather.3.cloned.1.call-done = bf16[4,1536,128]{2,1,0:T(8,128)(2,1)} async-done(((bf16[1,1536,128]{2,1,0:T(8,128)(2,1)}), bf16[4,1536,128]{2,1,0:T(8,128)(2,1)}) %all-gather.3.cloned.1.call-update) | async-done | bytes 1572880 | tf_op jit(solution)/shard_map/all_gather | solution.py:23
  92.5 39.9 %all-gather.5.cloned.1.call-done = bf16[8,1536,128]{2,1,0:T(8,128)(2,1)} async-done(((bf16[1,1536,128]{2,1,0:T(8,128)(2,1)}), bf16[8,1536,128]{2,1,0:T(8,128)(2,1)}) %all-gather.5.cloned.1.call-update) | async-done | bytes 3145744 | tf_op jit(solution)/shard_map/all_gather | solution.py:26
  132.4 5.5 %bitcast_subtract_fusion = f32[1,1,8,4,128,128]{4,5,2,3,1,0:T(8,128)} fusion(f32[1,1,8,4,128,128]{4,5,2,3,1,0:T(8,128)S(1)} %copy.16, bf16[8,1536,128]{2,1,0:T(8,128)(2,1)} %all-gather.5.cloned.1.call-done, bf16[4,1536,128]{2,1,0:T(8,128)(2,1)} %all-gather.3.cloned.1.call-done), kind=kOutput, calls=%fused_computation.7 | convolution fusion | flops 1611137024 | bytes 8912896 | tf_op jit(solution)/shard_map/aik,bil->abkl/dot_general | solution.py:24
  137.9 2.9 %copy.17 = f32[1,1,8,4,128,128]{5,4,3,2,1,0:T(8,128)} copy(f32[1,1,8,4,128,128]{4,5,2,3,1,0:T(8,128)} %bitcast_subtract_fusion) | data formatting | bytes 4194304 | tf_op jit(solution)/shard_map/sub | solution.py:30
  (4 shorter events, 0.0 us)
Async XLA Ops:
  6.5 18.9 %all-to-all-start = ((bf16[8,192,128]{2,1,0:T(8,128)(2,1)}), bf16[8,192,128]{2,1,0:T(8,128)(2,1)S(1)}, u32[]{:S(2)}, u32[]{:S(2)}) async-start(bf16[8,192,128]{2,1,0:T(8,128)(2,1)} %param.5), calls=%async_computation | async-start | bytes 786432 | tf_op jit(solution)/shard_map/all_to_all | solution.py:13
  25.4 8.6 %copy-start = (s32[32]{0:T(128)S(1)}, s32[32]{0:T(128)}, u32[]{:S(2)}) copy-start(s32[32]{0:T(128)} %param.8) | copy-start | bytes 388
  30.4 17.0 %all-to-all-start.1 = ((bf16[32,48,128]{2,1,0:T(8,128)(2,1)}), bf16[32,48,128]{2,1,0:T(8,128)(2,1)S(1)}, u32[]{:S(2)}, u32[]{:S(2)}) async-start(bf16[32,48,128]{2,1,0:T(8,128)(2,1)} %bitcast.4), calls=%async_computation.1 | async-start | bytes 786432 | tf_op jit(solution)/shard_map/all_to_all | solution.py:19
  33.9 58.6 %all-gather.3.cloned.1.call-start = ((), (), s32[]{:S(2)}) async-start(), calls=%async_computation.3 | async-start | bytes 1966080 | tf_op jit(solution)/shard_map/all_gather | solution.py:23
  63.9 68.5 %all-gather.5.cloned.1.call-start = ((), (), s32[]{:S(2)}) async-start(), calls=%async_computation.4 | async-start | bytes 3538944 | tf_op jit(solution)/shard_map/all_gather | solution.py:26
Sparse Core Ops, SparseCore 0:
  64.0 28.4 all-gather.2
  94.1 38.2 all-gather.4
where the time goes:
time: 148 us
  waiting for transfers between devices  91.7 us (62%)
  blocking collectives  15.8 us (11%)
  between operations  14.1 us (10%)
  starting transfers between devices  9.97 us (7%)
  matrix products  9.54 us (6%)
  local copies, waits for them, and re-layouts  6.37 us (4%)
    all_gather x1, waiting for transfers between devices, body(): lax.all_gather(held, 'col', axis=0, tiled=True)  39.9 us
    all_gather x1, waiting for transfers between devices, body(): column_set = lax.all_gather(held, 'row', axis=0, tiled=True)  25.9 us
    all_to_all x1, blocking collectives, body(): lax.all_to_all(moved, ('row', 'col'), split_axis=0, concat_axis=0, tiled=...  15.8 us
    all_to_all x1, waiting for transfers between devices, body(): lax.all_to_all(pieces, ('row', 'col'), split_axis=0, concat_axis=0, tiled...  13.3 us
    all_to_all x1, waiting for transfers between devices, body(): lax.all_to_all(panel_right, 'col', split_axis=0, concat_axis=1, tiled=True)  11.9 us
    all_to_all x1, starting transfers between devices, body(): lax.all_to_all(panel_right, 'col', split_axis=0, concat_axis=1, tiled=True)  6.35 us
    dot_general x1, matrix products, body(): jnp.einsum('aik,bil->abkl', lax.all_gather(held, 'col', axis=0, tiled=Tru...  5.51 us
    dot_general x1, matrix products, body(): jnp.einsum('ij,bjk->bik', factor_inverse, whole, preferred_element_type=j...  4.03 us
  transfers between devices with their start and end apart: 4, of which 4 were waited for; matrix products, arithmetic and copies ran while one was open for 1% of the time, Pallas kernels for 0%

commit v1 on v0

--- a/solution.py
+++ b/solution.py
@@ -10,7 +10,12 @@
     devices = n_row * n_col
     order = factor_inverse.shape[0]
     width = panel_right.shape[2]
-    whole = lax.all_to_all(panel_right, "col", split_axis=0, concat_axis=1, tiled=True)
+    whole = jnp.concatenate(
+        lax.all_to_all(
+            jnp.stack(jnp.split(panel_right, lax.axis_size("col"), axis=0)), "col", 0, 0
+        ),
+        axis=1,
+    )
     solved = jnp.einsum("ij,bjk->bik", factor_inverse, whole, preferred_element_type=jnp.float32)
     column = lax.broadcasted_iota(jnp.int32, (1, 1, width), 2)
     keep = column < ranks.reshape(1, 1, 1)

time: 148 us -> 160 us (1.081)
  local copies, waits for them, and re-layouts: 6.37 us -> 17.7 us
    unnamed x3 -> x10, local copies, waits for them, and re-layouts: 1.94 us -> 11.9 us
where the time goes in v1:
time: 160 us; the launch traced here: 159 us
  waiting for transfers between devices  91.7 us (57%)
  local copies, waits for them, and re-layouts  17.7 us (11%)
  blocking collectives  15.8 us (10%)
  between operations  14.1 us (9%)
  starting transfers between devices  9.97 us (6%)
  matrix products  9.54 us (6%)
    all_gather x1, waiting for transfers between devices, body(): lax.all_gather(held, 'col', axis=0, tiled=True)  39.9 us
    all_gather x1, waiting for transfers between devices, body(): column_set = lax.all_gather(held, 'row', axis=0, tiled=True)  25.9 us
    all_to_all x1, blocking collectives, body(): lax.all_to_all(moved, ('row', 'col'), split_axis=0, concat_axis=0, tiled=...  15.8 us
    all_to_all x1, waiting for transfers between devices, body(): lax.all_to_all(pieces, ('row', 'col'), split_axis=0, concat_axis=0, tiled...  13.3 us
    unnamed x10, local copies, waits for them, and re-layouts  11.9 us
    all_to_all x1, waiting for transfers between devices, body(): lax.all_to_all(jnp.stack(jnp.split(panel_right, lax.axis_size('col'), axi...  11.9 us
    all_to_all x1, starting transfers between devices, body(): lax.all_to_all(jnp.stack(jnp.split(panel_right, lax.axis_size('col'), axi...  6.35 us
    dot_general x1, matrix products, body(): jnp.einsum('aik,bil->abkl', lax.all_gather(held, 'col', axis=0, tiled=Tru...  5.51 us
  transfers between devices with their start and end apart: 4, of which 4 were waited for; matrix products, arithmetic and copies ran while one was open for 1% of the time, Pallas kernels for 0%

profile of v1, /device:TPU:0, one launch (start us, length us, event | category | flops | bytes accessed | tf_op | source)
XLA Modules:
  0.0 159.0 jit_solution(2959239194299270479)
XLA Ops:
  6.5 1.4 bitcast_dynamic-update-slice_fusion.7
  8.0 1.4 bitcast_dynamic-update-slice_fusion.6
  9.4 1.4 bitcast_dynamic-update-slice_fusion.5
  10.8 1.4 bitcast_dynamic-update-slice_fusion.4
  12.2 1.4 bitcast_dynamic-update-slice_fusion.3
  13.6 1.4 bitcast_dynamic-update-slice_fusion.2
  15.1 1.4 bitcast_dynamic-update-slice_fusion.1
  16.5 1.4 bitcast_dynamic-update-slice_fusion
  17.9 6.4 %all-to-all-start = ((bf16[8,1,192,128]{3,2,1,0:T(8,128)(2,1)}), bf16[8,1,192,128]{3,2,1,0:T(8,128)(2,1)S(1)}, u32[]{:S(2)}, u32[]{:S(2)}) async-start(bf16[8,1,192,128]{3,2,1,0:T(8,128)(2,1)} %bitcast_dynamic-update-slice_fusion), calls=%async_computation | async-start | bytes 786432 | tf_op jit(solution)/shard_map/all_to_all | solution.py:14
  24.9 11.9 %all-to-all-done = bf16[8,1,192,128]{3,2,1,0:T(8,128)(2,1)S(1)} async-done(((bf16[8,1,192,128]{3,2,1,0:T(8,128)(2,1)}), bf16[8,1,192,128]{3,2,1,0:T(8,128)(2,1)S(1)}, u32[]{:S(2)}, u32[]{:S(2)}) %all-to-all-start) | async-done | bytes 393248 | tf_op jit(solution)/shard_map/all_to_all | solution.py:14
  36.8 4.0 %fusion.4 = bf16[1,1536,128]{1,2,0:T(8,128)(2,1)S(1)} fusion(bf16[1536,128]{1,0:T(8,128)(2,1)S(1)} %bitcast.49, bf16[1536,1536]{1,0:T(8,128)(2,1)} %param.6, pred[128]{0:T(512)(128)(4,1)S(1)} %iota_compare_fusion), kind=kOutput, calls=%fused_computation.6 | convolution fusion | flops 604372992 | bytes 5505152 | tf_op jit(solution)/shard_map/ij,bjk->bik/dot_general | solution.py:19
  40.8 0.9 copy.14
  41.7 3.5 %all-to-all-start.1 = ((bf16[32,48,128]{2,1,0:T(8,128)(2,1)}), bf16[32,48,128]{2,1,0:T(8,128)(2,1)S(1)}, u32[]{:S(2)}, u32[]{:S(2)}) async-start(bf16[32,48,128]{2,1,0:T(8,128)(2,1)} %bitcast.12), calls=%async_computation.1 | async-start | bytes 786432 | tf_op jit(solution)/shard_map/all_to_all | solution.py:24
  45.4 13.3 %all-to-all-done.1 = bf16[32,48,128]{2,1,0:T(8,128)(2,1)S(1)} async-done(((bf16[32,48,128]{2,1,0:T(8,128)(2,1)}), bf16[32,48,128]{2,1,0:T(8,128)(2,1)S(1)}, u32[]{:S(2)}, u32[]{:S(2)}) %all-to-all-start.1) | async-done | bytes 393248 | tf_op jit(solution)/shard_map/all_to_all | solution.py:24
  58.7 0.6 gather_fusion
  59.3 0.1 broadcast_select_fusion
  59.4 15.8 %all_to_all.15 = bf16[32,48,128]{2,1,0:T(8,128)(2,1)} all-to-all(bf16[32,48,128]{2,1,0:T(8,128)(2,1)S(1)} %broadcast_select_fusion), channel_id=1, replica_groups=mesh['row'=4,'col'=8] {'row','col'}, dimensions={0} | all-to-all | bytes 786432 | tf_op jit(solution)/shard_map/all_to_all | solution.py:26
  75.3 0.0 all-gather.5.cloned.1.call-start
  75.3 0.7 all-gather.5.cloned.1.call-update
  76.0 1.9 %copy.16 = f32[1,1,8,4,128,128]{4,5,2,3,1,0:T(8,128)S(1)} copy(f32[1,1,8,4,128,128]{5,4,3,2,1,0:T(8,128)} %param.9) | data formatting | bytes 4194304 | tf_op args[4]
  78.0 25.9 %all-gather.3.cloned.1.call-done = bf16[4,1536,128]{2,1,0:T(8,128)(2,1)} async-done(((bf16[1,1536,128]{2,1,0:T(8,128)(2,1)}), bf16[4,1536,128]{2,1,0:T(8,128)(2,1)}) %all-gather.3.cloned.1.call-update) | async-done | bytes 1572880 | tf_op jit(solution)/shard_map/all_gather | solution.py:28
  103.9 39.9 %all-gather.5.cloned.1.call-done = bf16[8,1536,128]{2,1,0:T(8,128)(2,1)} async-done(((bf16[1,1536,128]{2,1,0:T(8,128)(2,1)}), bf16[8,1536,128]{2,1,0:T(8,128)(2,1)}) %all-gather.5.cloned.1.call-update) | async-done | bytes 3145744 | tf_op jit(solution)/shard_map/all_gather | solution.py:31
  143.8 5.5 %bitcast_subtract_fusion = f32[1,1,8,4,128,128]{4,5,2,3,1,0:T(8,128)} fusion(f32[1,1,8,4,128,128]{4,5,2,3,1,0:T(8,128)S(1)} %copy.16, bf16[8,1536,128]{2,1,0:T(8,128)(2,1)} %all-gather.5.cloned.1.call-done, bf16[4,1536,128]{2,1,0:T(8,128)(2,1)} %all-gather.3.cloned.1.call-done), kind=kOutput, calls=%fused_computation.7 | convolution fusion | flops 1611137024 | bytes 8912896 | tf_op jit(solution)/shard_map/aik,bil->abkl/dot_general | solution.py:29
  149.3 2.9 %copy.17 = f32[1,1,8,4,128,128]{5,4,3,2,1,0:T(8,128)} copy(f32[1,1,8,4,128,128]{4,5,2,3,1,0:T(8,128)} %bitcast_subtract_fusion) | data formatting | bytes 4194304 | tf_op jit(solution)/shard_map/sub | solution.py:35
  (8 shorter events, 0.1 us)
Async XLA Ops:
  17.9 18.9 %all-to-all-start = ((bf16[8,1,192,128]{3,2,1,0:T(8,128)(2,1)}), bf16[8,1,192,128]{3,2,1,0:T(8,128)(2,1)S(1)}, u32[]{:S(2)}, u32[]{:S(2)}) async-start(bf16[8,1,192,128]{3,2,1,0:T(8,128)(2,1)} %bitcast_dynamic-update-slice_fusion), calls=%async_computation | async-start | bytes 786432 | tf_op jit(solution)/shard_map/all_to_all | solution.py:14
  36.8 8.6 %copy-start = (s32[32]{0:T(128)S(1)}, s32[32]{0:T(128)}, u32[]{:S(2)}) copy-start(s32[32]{0:T(128)} %param.8) | copy-start | bytes 388
  41.7 17.0 %all-to-all-start.1 = ((bf16[32,48,128]{2,1,0:T(8,128)(2,1)}), bf16[32,48,128]{2,1,0:T(8,128)(2,1)S(1)}, u32[]{:S(2)}, u32[]{:S(2)}) async-start(bf16[32,48,128]{2,1,0:T(8,128)(2,1)} %bitcast.12), calls=%async_computation.1 | async-start | bytes 786432 | tf_op jit(solution)/shard_map/all_to_all | solution.py:24
  45.3 58.6 %all-gather.3.cloned.1.call-start = ((), (), s32[]{:S(2)}) async-start(), calls=%async_computation.3 | async-start | bytes 1966080 | tf_op jit(solution)/shard_map/all_gather | solution.py:28
  75.3 68.5 %all-gather.5.cloned.1.call-start = ((), (), s32[]{:S(2)}) async-start(), calls=%async_computation.4 | async-start | bytes 3538944 | tf_op jit(solution)/shard_map/all_gather | solution.py:31
Sparse Core Ops, SparseCore 0:
  75.4 28.4 all-gather.2
  105.5 38.2 all-gather.4
